TPU v7x, 512 devices: a whole 4x8x8 slice. The times are simulated.
512 devices in a mesh: gx: 16 (over z, core), gy: 8 (over y), gz: 4 (over x).
Axes of the slice: x: 4, y: 8, z: 8, core: 2. Of those that a mesh axis runs over, the one named last changes fastest.
Arguments:
- snapshot: float32 [512, 1280, 512], P('gx', 'gy', 'gz'), may hold values from -40 to 40
Outputs:
- basis: float32 [512, 128], P('gx')
- core: float32 [128, 1280, 512], P('gx', 'gy', 'gz')
All inputs are finite; a program needn't handle non-finite values.
Results may differ from a plain program's by a relative error of at most 0.0002.
Values sent between devices are 32-bit elements; how exact they have to be, the bound alone decides.
A program may use at most 64 MiB of HBM per device.

v0:
```python
import jax
import jax.numpy as jnp
from jax import lax
from jax.sharding import PartitionSpec as P

RANK = 128
ITERS = 2


def product(left, right):
    return jnp.dot(left, right, precision=lax.Precision.HIGHEST, preferred_element_type=jnp.float32)


def orthonormal(matrix):
    lower = jnp.linalg.cholesky(product(matrix.T, matrix))
    return jax.scipy.linalg.solve_triangular(lower, matrix.T, lower=True).T


def local(snapshot):
    xlocal, ylocal, zlocal = snapshot.shape
    flat = snapshot.reshape(xlocal, ylocal * zlocal)
    fibres = lax.all_to_all(flat, "gx", split_axis=1, concat_axis=0, tiled=True)
    gram = product(fibres, fibres.T)
    factor = jnp.linalg.cholesky(lax.psum(gram, ("gx", "gy", "gz")))
    basis = orthonormal(factor[:, :RANK])
    for step in range(ITERS):
        basis = orthonormal(product(factor, product(factor.T, basis)))
    groups = lax.axis_size("gx")
    own_rows = basis.shape[0] // groups
    mine = lax.dynamic_slice_in_dim(basis, lax.axis_index("gx") * own_rows, own_rows, 0)
    projected = product(basis.T, fibres)
    returned = lax.all_to_all(projected, "gx", split_axis=0, concat_axis=1, tiled=True)
    return (mine, returned.reshape(RANK // groups, ylocal, zlocal))


def solution(mesh):
    in_specs = (P("gx", "gy", "gz"),)
    out_specs = (P("gx", None), P("gx", "gy", "gz"))
    return jax.shard_map(local, mesh=mesh, in_specs=in_specs, out_specs=out_specs, check_vma=False)
```

profile of v0, /device:TPU:1, one launch (start us, length us, event | category | flops | bytes accessed | tf_op | source)
XLA Modules:
  0.0 580.8 jit_solution(15275635226569136335)
XLA Ops:
  7.2 0.0 all-reduce.3.cloned.1.call-start
  7.2 2.6 all_to_all.24
  9.8 1.5 copy.10
  11.3 73.8 %all_to_all.32 = f32[32,16,1280]{2,0,1:T(8,128)S(1)} all-to-all(f32[32,16,1280]{2,0,1:T(8,128)S(1)} %copy.10), channel_id=1, replica_groups=mesh['gx'=16,'gy'=8,'gz'=4] {'gx'}, dimensions={1} | all-to-all | bytes 5242880 | tf_op jit(solution)/shard_map/all_to_all | solution.py:22
  85.1 5.3 fusion.50
  90.5 0.0 all-reduce.3.cloned.1.call-update
  90.5 272.2 %all-reduce.3.cloned.1.call-done = f32[512,512]{0,1:T(8,128)} async-done(((f32[512,512]{0,1:T(8,128)}), f32[512,512]{0,1:T(8,128)}) %all-reduce.3.cloned.1.call-update) | async-done | bytes 1048592 | tf_op jit(solution)/shard_map/psum | solution.py:24
  362.7 2.6 copy.12
  365.2 1.8 fusion
  367.0 1.0 copy-done.3
  368.0 11.7 %cholesky.120 = f32[128,128]{1,0:T(8,128)S(1)} custom-call(f32[128,128]{1,0:T(8,128)S(1)} %cholesky.356), custom_call_target="Cholesky" | custom-call | tf_op jit(solution)/shard_map/jit(cholesky)/cholesky | solution.py:24
  379.8 9.8 %custom-call.32 = f32[1,128,128]{1,2,0:T(8,128)S(1)} custom-call(f32[1,128,128]{2,1,0:T(8,128)S(1)} %get-tuple-element.17), custom_call_target="InvertDiagBlocksLowerTriangular" | custom-call | tf_op jit(solution)/shard_map/jit(cholesky)/cholesky | solution.py:24
  389.6 1.2 cholesky.251
  390.7 2.0 constant_dynamic-update-slice_fusion.2
  392.7 1.2 convolution_subtract_fusion
  394.0 11.9 %cholesky.244 = f32[128,128]{1,0:T(8,128)S(1)} custom-call(f32[128,128]{1,0:T(8,128)S(1)} %cholesky.360), custom_call_target="Cholesky" | custom-call | tf_op jit(solution)/shard_map/jit(cholesky)/cholesky | solution.py:24
  405.9 0.6 fusion.45
  406.5 9.8 %custom-call.33 = f32[1,128,128]{1,2,0:T(8,128)S(1)} custom-call(f32[1,128,128]{2,1,0:T(8,128)S(1)} %get-tuple-element.14), custom_call_target="InvertDiagBlocksLowerTriangular" | custom-call | tf_op jit(solution)/shard_map/jit(cholesky)/cholesky | solution.py:24
  416.3 0.9 convolution_dynamic-update-slice_fusion
  417.3 1.4 convolution_subtract_fusion.1
  418.7 11.7 %cholesky.265 = f32[128,128]{1,0:T(8,128)S(1)} custom-call(f32[128,128]{1,0:T(8,128)S(1)} %cholesky.365), custom_call_target="Cholesky" | custom-call | tf_op jit(solution)/shard_map/jit(cholesky)/cholesky | solution.py:24
  430.4 0.6 fusion.46
  431.1 0.6 compare_reduce_fusion.4
  431.7 10.2 %custom-call.34 = f32[1,128,128]{1,2,0:T(8,128)S(1)} custom-call(f32[1,128,128]{2,1,0:T(8,128)S(1)} %get-tuple-element.11), custom_call_target="InvertDiagBlocksLowerTriangular" | custom-call | tf_op jit(solution)/shard_map/jit(cholesky)/cholesky | solution.py:24
  441.9 0.8 convolution_dynamic-update-slice_fusion.1
  442.7 1.4 convolution_subtract_fusion.2
  444.2 11.7 %cholesky.282 = f32[128,128]{1,0:T(8,128)S(1)} custom-call(f32[128,128]{1,0:T(8,128)S(1)} %convolution_subtract_fusion.2), custom_call_target="Cholesky" | custom-call | tf_op jit(solution)/shard_map/jit(cholesky)/cholesky | solution.py:24
  455.9 0.7 fusion.47
  456.5 0.7 compare_reduce_fusion.3
  457.2 0.6 compare_reduce_fusion.5
  460.5 1.4 select_select_fusion
  461.9 1.0 copy-done
  462.8 0.6 fusion.11
  463.4 0.1 copy.13
  463.5 11.7 %cholesky.325 = f32[128,128]{1,0:T(8,128)S(1)} custom-call(f32[128,128]{1,0:T(8,128)S(1)} %fusion.28), custom_call_target="Cholesky" | custom-call | tf_op jit(solution)/shard_map/jit(cholesky)/cholesky | solution.py:15
  475.3 0.6 compare_reduce_fusion.2
  475.9 0.7 fusion.18
  476.6 9.8 %custom-call.37 = f32[1,128,128]{1,2,0:T(8,128)S(1)} custom-call(f32[1,128,128]{2,1,0:T(8,128)S(1)} %fusion.18), custom_call_target="InvertDiagBlocksLowerTriangular" | custom-call | tf_op jit(solution)/shard_map/jit(_solve_triangular)/triangular_solve | solution.py:16
  486.4 1.5 fusion.8
  487.9 3.2 fusion.51
  491.1 1.0 fusion.52
  492.1 0.6 fusion.53
  492.7 0.1 copy.14
  492.8 11.7 %cholesky.336 = f32[128,128]{1,0:T(8,128)S(1)} custom-call(f32[128,128]{1,0:T(8,128)S(1)} %fusion.26), custom_call_target="Cholesky" | custom-call | tf_op jit(solution)/shard_map/jit(cholesky)/cholesky | solution.py:15
  504.6 0.6 compare_reduce_fusion.1
  505.2 0.7 fusion.19
  505.9 9.8 %custom-call.38 = f32[1,128,128]{1,2,0:T(8,128)S(1)} custom-call(f32[1,128,128]{2,1,0:T(8,128)S(1)} %fusion.19), custom_call_target="InvertDiagBlocksLowerTriangular" | custom-call | tf_op jit(solution)/shard_map/jit(_solve_triangular)/triangular_solve | solution.py:16
  515.7 0.4 fusion.6
  516.1 3.0 fusion.54
  519.2 1.0 fusion.55
  520.1 0.8 fusion.56
  520.9 0.1 copy.15
  521.1 11.7 %cholesky.347 = f32[128,128]{1,0:T(8,128)S(1)} custom-call(f32[128,128]{1,0:T(8,128)S(1)} %fusion.24), custom_call_target="Cholesky" | custom-call | tf_op jit(solution)/shard_map/jit(cholesky)/cholesky | solution.py:15
  532.8 0.6 compare_reduce_fusion
  533.5 0.7 fusion.20
  534.1 9.8 %custom-call.39 = f32[1,128,128]{1,2,0:T(8,128)S(1)} custom-call(f32[1,128,128]{2,1,0:T(8,128)S(1)} %fusion.20), custom_call_target="InvertDiagBlocksLowerTriangular" | custom-call | tf_op jit(solution)/shard_map/jit(_solve_triangular)/triangular_solve | solution.py:16
  543.9 0.4 fusion.4
  544.4 2.3 fusion.2
  546.6 6.0 %all-to-all-start.1 = ((f32[16,8,1280]{2,1,0:T(8,128)}), f32[16,8,1280]{2,1,0:T(8,128)S(1)}, u32[]{:S(2)}, u32[]{:S(2)}) async-start(f32[16,8,1280]{2,1,0:T(8,128)} %fusion.2), calls=%async_computation.1 | async-start | bytes 1310720 | tf_op jit(solution)/shard_map/all_to_all | solution.py:32
  552.7 0.1 dynamic-slice_bitcast_fusion
  552.8 0.7 copy.17
  553.4 19.2 %all-to-all-done.1 = f32[16,8,1280]{2,1,0:T(8,128)S(1)} async-done(((f32[16,8,1280]{2,1,0:T(8,128)}), f32[16,8,1280]{2,1,0:T(8,128)S(1)}, u32[]{:S(2)}, u32[]{:S(2)}) %all-to-all-start.1) | async-done | bytes 655392 | tf_op jit(solution)/shard_map/all_to_all | solution.py:32
  572.6 0.2 copy.16
  572.8 0.9 reshape.52
  (16 shorter events, 0.2 us)
Async XLA Ops:
  7.2 355.5 %all-reduce.3.cloned.1.call-start = ((), (), s32[]{:S(2)}) async-start(), calls=%async_computation.2 | async-start | bytes 2097152 | tf_op jit(solution)/shard_map/psum | solution.py:24
  367.0 1.0 copy-start.3
  461.8 1.0 copy-start
  486.4 4.7 copy-start.1
  515.7 3.5 copy-start.2
  546.6 26.0 %all-to-all-start.1 = ((f32[16,8,1280]{2,1,0:T(8,128)}), f32[16,8,1280]{2,1,0:T(8,128)S(1)}, u32[]{:S(2)}, u32[]{:S(2)}) async-start(f32[16,8,1280]{2,1,0:T(8,128)} %fusion.2), calls=%async_computation.1 | async-start | bytes 1310720 | tf_op jit(solution)/shard_map/all_to_all | solution.py:32
Sparse Core Ops, SparseCore 0:
  90.6 272.0 all-reduce.2
where the time goes:
time: 584 us; the launch traced here: 581 us
  waiting for transfers between devices  291 us (50%)
  other arithmetic  153 us (26%)
  blocking collectives  73.8 us (13%)
  matrix products  27.9 us (5%)
  between operations  17.2 us (3%)
  local copies, waits for them, and re-layouts  12 us (2%)
  starting transfers between devices  6.08 us (1%)
    psum x1, waiting for transfers between devices, local(): factor = jnp.linalg.cholesky(lax.psum(gram, ('gx', 'gy', 'gz')))  272 us
    another operation x14, other arithmetic, local(): factor = jnp.linalg.cholesky(lax.psum(gram, ('gx', 'gy', 'gz')))  80.8 us
    all_to_all x1, blocking collectives, local(): fibres = lax.all_to_all(flat, 'gx', split_axis=1, concat_axis=0, tiled=True)  73.8 us
    another operation x9, other arithmetic, orthonormal(): lower = jnp.linalg.cholesky(product(matrix.T, matrix))  37.2 us
    another operation x6, other arithmetic, orthonormal(): return jax.scipy.linalg.solve_triangular(lower, matrix.T, lower=True).T  31.4 us
    all_to_all x1, waiting for transfers between devices, local(): lax.all_to_all(projected, 'gx', split_axis=0, concat_axis=1, tiled=True)  19.2 us
    dot_general x9, matrix products, product(): jnp.dot(left, right, precision=lax.Precision.HIGHEST, preferred_element_t...  17.8 us
  transfers between devices with their start and end apart: 2, of which 2 were waited for; matrix products, arithmetic and copies ran while one was open for 0% of the time, Pallas kernels for 0%

commit v1 on v0

--- a/solution.py
+++ b/solution.py
@@ -19,7 +19,9 @@
 def local(snapshot):
     xlocal, ylocal, zlocal = snapshot.shape
     flat = snapshot.reshape(xlocal, ylocal * zlocal)
-    fibres = lax.all_to_all(flat, "gx", split_axis=1, concat_axis=0, tiled=True)
+    fibres = jnp.concatenate(
+        lax.all_to_all(jnp.stack(jnp.split(flat, lax.axis_size("gx"), axis=1)), "gx", 0, 0), axis=0
+    )
     gram = product(fibres, fibres.T)
     factor = jnp.linalg.cholesky(lax.psum(gram, ("gx", "gy", "gz")))
     basis = orthonormal(factor[:, :RANK])

time: 584 us -> 583 us (level)
  no operation moved by 1% of the time
where the time goes in v1:
time: 583 us; the launch traced here: 580 us
  waiting for transfers between devices  291 us (50%)
  other arithmetic  153 us (26%)
  blocking collectives  73.8 us (13%)
  matrix products  27.9 us (5%)
  between operations  17.3 us (3%)
  local copies, waits for them, and re-layouts  11.4 us (2%)
  starting transfers between devices  6.06 us (1%)
    psum x1, waiting for transfers between devices, local(): factor = jnp.linalg.cholesky(lax.psum(gram, ('gx', 'gy', 'gz')))  272 us
    another operation x14, other arithmetic, local(): factor = jnp.linalg.cholesky(lax.psum(gram, ('gx', 'gy', 'gz')))  80.8 us
    all_to_all x1, blocking collectives, local(): lax.all_to_all(jnp.stack(jnp.split(flat, lax.axis_size('gx'), axis=1)), '...  73.8 us
    another operation x9, other arithmetic, orthonormal(): lower = jnp.linalg.cholesky(product(matrix.T, matrix))  37.2 us
    another operation x6, other arithmetic, orthonormal(): return jax.scipy.linalg.solve_triangular(lower, matrix.T, lower=True).T  31.4 us
    all_to_all x1, waiting for transfers between devices, local(): lax.all_to_all(projected, 'gx', split_axis=0, concat_axis=1, tiled=True)  19.2 us
    dot_general x9, matrix products, product(): jnp.dot(left, right, precision=lax.Precision.HIGHEST, preferred_element_t...  17.8 us
  transfers between devices with their start and end apart: 2, of which 2 were waited for; matrix products, arithmetic and copies ran while one was open for 0% of the time, Pallas kernels for 0%

profile of v1, /device:TPU:1, one launch (start us, length us, event | category | flops | bytes accessed | tf_op | source)
XLA Modules:
  0.0 580.3 jit_solution(9135855639951845390)
XLA Ops:
  7.2 0.0 all-reduce.3.cloned.1.call-start
  7.2 3.3 copy.19
  10.8 73.8 %all_to_all.18 = f32[16,32,1280]{2,1,0:T(8,128)S(1)} all-to-all(f32[16,32,1280]{2,1,0:T(8,128)S(1)} %fusion.16), channel_id=1, replica_groups=mesh['gx'=16,'gy'=8,'gz'=4] {'gx'}, dimensions={0} | all-to-all | bytes 5242880 | tf_op jit(solution)/shard_map/all_to_all | solution.py:23
  84.6 5.3 fusion.66
  89.9 0.0 all-reduce.3.cloned.1.call-update
  89.9 272.3 %all-reduce.3.cloned.1.call-done = f32[512,512]{0,1:T(8,128)} async-done(((f32[512,512]{0,1:T(8,128)}), f32[512,512]{0,1:T(8,128)}) %all-reduce.3.cloned.1.call-update) | async-done | bytes 1048592 | tf_op jit(solution)/shard_map/psum | solution.py:26
  362.2 2.6 copy.10
  364.8 1.8 fusion
  366.6 0.0 copy-start.3
  366.6 1.0 copy-done.3
  367.6 11.7 %cholesky.120 = f32[128,128]{1,0:T(8,128)S(1)} custom-call(f32[128,128]{1,0:T(8,128)S(1)} %cholesky.356), custom_call_target="Cholesky" | custom-call | tf_op jit(solution)/shard_map/jit(cholesky)/cholesky | solution.py:26
  379.3 1.2 cholesky.251
  380.5 9.8 %custom-call.32 = f32[1,128,128]{1,2,0:T(8,128)S(1)} custom-call(f32[1,128,128]{2,1,0:T(8,128)S(1)} %get-tuple-element.17), custom_call_target="InvertDiagBlocksLowerTriangular" | custom-call | tf_op jit(solution)/shard_map/jit(cholesky)/cholesky | solution.py:26
  390.3 2.0 constant_dynamic-update-slice_fusion.2
  392.3 1.3 convolution_subtract_fusion
  393.5 11.9 %cholesky.244 = f32[128,128]{1,0:T(8,128)S(1)} custom-call(f32[128,128]{1,0:T(8,128)S(1)} %cholesky.360), custom_call_target="Cholesky" | custom-call | tf_op jit(solution)/shard_map/jit(cholesky)/cholesky | solution.py:26
  405.4 0.6 fusion.61
  406.1 9.8 %custom-call.33 = f32[1,128,128]{1,2,0:T(8,128)S(1)} custom-call(f32[1,128,128]{2,1,0:T(8,128)S(1)} %get-tuple-element.14), custom_call_target="InvertDiagBlocksLowerTriangular" | custom-call | tf_op jit(solution)/shard_map/jit(cholesky)/cholesky | solution.py:26
  415.9 0.9 convolution_dynamic-update-slice_fusion
  416.8 1.4 convolution_subtract_fusion.1
  418.3 11.7 %cholesky.265 = f32[128,128]{1,0:T(8,128)S(1)} custom-call(f32[128,128]{1,0:T(8,128)S(1)} %cholesky.365), custom_call_target="Cholesky" | custom-call | tf_op jit(solution)/shard_map/jit(cholesky)/cholesky | solution.py:26
  430.0 0.6 fusion.62
  430.6 0.6 compare_reduce_fusion.4
  431.3 10.2 %custom-call.34 = f32[1,128,128]{1,2,0:T(8,128)S(1)} custom-call(f32[1,128,128]{2,1,0:T(8,128)S(1)} %get-tuple-element.11), custom_call_target="InvertDiagBlocksLowerTriangular" | custom-call | tf_op jit(solution)/shard_map/jit(cholesky)/cholesky | solution.py:26
  441.4 0.8 convolution_dynamic-update-slice_fusion.1
  442.3 1.4 convolution_subtract_fusion.2
  443.7 11.7 %cholesky.282 = f32[128,128]{1,0:T(8,128)S(1)} custom-call(f32[128,128]{1,0:T(8,128)S(1)} %convolution_subtract_fusion.2), custom_call_target="Cholesky" | custom-call | tf_op jit(solution)/shard_map/jit(cholesky)/cholesky | solution.py:26
  455.4 0.7 fusion.63
  456.1 0.7 compare_reduce_fusion.3
  456.8 0.6 compare_reduce_fusion.5
  460.0 1.4 select_select_fusion
  461.4 1.0 copy-done
  462.4 0.6 fusion.11
  463.0 0.1 copy.11
  463.1 11.7 %cholesky.325 = f32[128,128]{1,0:T(8,128)S(1)} custom-call(f32[128,128]{1,0:T(8,128)S(1)} %fusion.44), custom_call_target="Cholesky" | custom-call | tf_op jit(solution)/shard_map/jit(cholesky)/cholesky | solution.py:15
  474.8 0.6 compare_reduce_fusion.2
  475.5 0.7 fusion.34
  476.2 9.8 %custom-call.37 = f32[1,128,128]{1,2,0:T(8,128)S(1)} custom-call(f32[1,128,128]{2,1,0:T(8,128)S(1)} %fusion.34), custom_call_target="InvertDiagBlocksLowerTriangular" | custom-call | tf_op jit(solution)/shard_map/jit(_solve_triangular)/triangular_solve | solution.py:16
  486.0 1.5 fusion.8
  487.4 3.2 fusion.67
  490.7 1.0 fusion.68
  491.6 0.6 fusion.69
  492.2 0.1 copy.12
  492.4 11.7 %cholesky.336 = f32[128,128]{1,0:T(8,128)S(1)} custom-call(f32[128,128]{1,0:T(8,128)S(1)} %fusion.42), custom_call_target="Cholesky" | custom-call | tf_op jit(solution)/shard_map/jit(cholesky)/cholesky | solution.py:15
  504.1 0.6 compare_reduce_fusion.1
  504.7 0.7 fusion.35
  505.4 9.8 %custom-call.38 = f32[1,128,128]{1,2,0:T(8,128)S(1)} custom-call(f32[1,128,128]{2,1,0:T(8,128)S(1)} %fusion.35), custom_call_target="InvertDiagBlocksLowerTriangular" | custom-call | tf_op jit(solution)/shard_map/jit(_solve_triangular)/triangular_solve | solution.py:16
  515.2 0.4 fusion.6
  515.7 3.0 fusion.70
  518.7 1.0 fusion.71
  519.7 0.8 fusion.72
  520.5 0.1 copy.13
  520.6 11.7 %cholesky.347 = f32[128,128]{1,0:T(8,128)S(1)} custom-call(f32[128,128]{1,0:T(8,128)S(1)} %fusion.40), custom_call_target="Cholesky" | custom-call | tf_op jit(solution)/shard_map/jit(cholesky)/cholesky | solution.py:15
  532.4 0.6 compare_reduce_fusion
  533.0 0.7 fusion.36
  533.7 9.8 %custom-call.39 = f32[1,128,128]{1,2,0:T(8,128)S(1)} custom-call(f32[1,128,128]{2,1,0:T(8,128)S(1)} %fusion.36), custom_call_target="InvertDiagBlocksLowerTriangular" | custom-call | tf_op jit(solution)/shard_map/jit(_solve_triangular)/triangular_solve | solution.py:16
  543.5 0.4 fusion.4
  543.9 2.3 fusion.2
  546.2 6.0 %all-to-all-start.1 = ((f32[16,8,1280]{2,1,0:T(8,128)}), f32[16,8,1280]{2,1,0:T(8,128)S(1)}, u32[]{:S(2)}, u32[]{:S(2)}) async-start(f32[16,8,1280]{2,1,0:T(8,128)} %fusion.2), calls=%async_computation.1 | async-start | bytes 1310720 | tf_op jit(solution)/shard_map/all_to_all | solution.py:34
  552.2 0.1 dynamic-slice_bitcast_fusion
  552.3 0.7 copy.15
  553.0 19.2 %all-to-all-done.1 = f32[16,8,1280]{2,1,0:T(8,128)S(1)} async-done(((f32[16,8,1280]{2,1,0:T(8,128)}), f32[16,8,1280]{2,1,0:T(8,128)S(1)}, u32[]{:S(2)}, u32[]{:S(2)}) %all-to-all-start.1) | async-done | bytes 655392 | tf_op jit(solution)/shard_map/all_to_all | solution.py:34
  572.2 0.2 copy.14
  572.4 0.9 reshape.55
  (31 shorter events, 0.4 us)
Async XLA Ops:
  7.2 355.0 %all-reduce.3.cloned.1.call-start = ((), (), s32[]{:S(2)}) async-start(), calls=%async_computation.2 | async-start | bytes 2097152 | tf_op jit(solution)/shard_map/psum | solution.py:26
  366.6 1.0 copy-start.3
  461.4 1.0 copy-start
  486.0 4.7 copy-start.1
  515.2 3.5 copy-start.2
  546.2 26.0 %all-to-all-start.1 = ((f32[16,8,1280]{2,1,0:T(8,128)}), f32[16,8,1280]{2,1,0:T(8,128)S(1)}, u32[]{:S(2)}, u32[]{:S(2)}) async-start(f32[16,8,1280]{2,1,0:T(8,128)} %fusion.2), calls=%async_computation.1 | async-start | bytes 1310720 | tf_op jit(solution)/shard_map/all_to_all | solution.py:34
Sparse Core Ops, SparseCore 0:
  90.1 272.0 all-reduce.2
